TPU v7x, 512 devices: a whole 4x8x8 slice. The times are simulated.
512 devices in a mesh: recv: 128 (over z, y_hi, x), tm: 4 (over y_lo, core).
Axes of the slice: x: 4, y: 8 (y_hi: 4, y_lo: 2; y = y_hi * 2 + y_lo), z: 8, core: 2. Of those that a mesh axis runs over, the one named last changes fastest.
Arguments:
- record: float32 [2048, 4096], P('recv', 'tm')
- source_channels: int32 [16], replicated, may hold values from 0 to 2047, as said below
- valid_mask: int32 [2048, 4], P('recv', 'tm'), may hold values 0 or 1
Outputs:
- lag_stack: float32 [16, 2048, 256], P('tm', 'recv')
Inputs may be any that keep to these rules, and one draw needn't show every extreme that they name: `source_channels`: ascending and distinct; source s lies in channels s * 128 to (s + 1) * 128 - 1; the first is channel 0 and the last channel 2048 - 1.
All inputs are finite; a program needn't handle non-finite values. No bound on the sum of `valid_mask` on one device may be relied on, other than what follows from the above.
Results may differ from a plain program's by a relative error of at most 0.0001.
Values sent between devices are 32-bit elements; how exact they have to be, the bound alone decides.
A program may use at most 64 MiB of HBM per device.

v0:
```python
import jax
import jax.numpy as jnp
from jax import lax
from jax.sharding import PartitionSpec as P

SEGLEN = 2048
NF = 1024
LAGS = 256
SMOOTH = 64
NSRC = 16


def shifted(block, axis, distance):
    devices = range(lax.axis_size(axis))
    route = [(i - distance, i) for i in devices if i - distance in devices]
    return lax.ppermute(block, axis, route)


def angle_table(rows, cols, period):
    first = lax.broadcasted_iota(jnp.int32, (rows, cols), 0)
    second = lax.broadcasted_iota(jnp.int32, (rows, cols), 1)
    return (first * second % period).astype(jnp.float32) * (2.0 * jnp.pi / period)


def fourier(tapered):
    row_count = tapered.shape[0]
    low_len = 16
    high_len = SEGLEN // 16
    keep_len = NF // 16
    blocks = tapered.reshape(row_count, low_len, high_len)
    first_angle = angle_table(low_len, low_len, low_len)
    first_re = jnp.einsum(
        "rmn,mf->rfn", blocks, jnp.cos(first_angle), precision=lax.Precision.HIGHEST
    )
    first_im = jnp.einsum(
        "rmn,mf->rfn", blocks, -jnp.sin(first_angle), precision=lax.Precision.HIGHEST
    )
    twist_angle = angle_table(low_len, high_len, SEGLEN)
    twist_re = jnp.cos(twist_angle)
    twist_im = -jnp.sin(twist_angle)
    mid_re = first_re * twist_re - first_im * twist_im
    mid_im = first_re * twist_im + first_im * twist_re
    last_angle = angle_table(high_len, keep_len, high_len)
    last_re = jnp.cos(last_angle)
    last_im = -jnp.sin(last_angle)
    out_re = jnp.einsum(
        "rfn,ng->rgf", mid_re, last_re, precision=lax.Precision.HIGHEST
    ) - jnp.einsum("rfn,ng->rgf", mid_im, last_im, precision=lax.Precision.HIGHEST)
    out_im = jnp.einsum(
        "rfn,ng->rgf", mid_re, last_im, precision=lax.Precision.HIGHEST
    ) + jnp.einsum("rfn,ng->rgf", mid_im, last_re, precision=lax.Precision.HIGHEST)
    return (out_re.reshape(row_count, NF), out_im.reshape(row_count, NF))


def inverse_table():
    freq_idx = lax.broadcasted_iota(jnp.int32, (NF, LAGS), 0)
    lag_idx = (lax.broadcasted_iota(jnp.int32, (NF, LAGS), 1) - LAGS // 2) % SEGLEN
    angle = (freq_idx * lag_idx % SEGLEN).astype(jnp.float32) * (2.0 * jnp.pi / SEGLEN)
    factor = jnp.where(freq_idx == 0, 1.0, 2.0) / SEGLEN
    return jnp.concatenate([factor * jnp.cos(angle), -factor * jnp.sin(angle)], axis=0)


def whiten(segments):
    sample_idx = lax.broadcasted_iota(jnp.int32, (1, SEGLEN), 1).astype(jnp.float32)
    taper_weights = 0.5 - 0.5 * jnp.cos(2.0 * jnp.pi * sample_idx / SEGLEN)
    tapered = (segments - jnp.mean(segments, axis=1, keepdims=True)) * taper_weights
    spec_re, spec_im = fourier(tapered)
    power_spec = spec_re * spec_re + spec_im * spec_im
    zero_init = jnp.zeros((), jnp.float32)
    counts = lax.reduce_window(
        jnp.ones((1, NF), jnp.float32),
        zero_init,
        lax.add,
        (1, 2 * SMOOTH + 1),
        (1, 1),
        [(0, 0), (SMOOTH, SMOOTH)],
    )
    smoothed = (
        lax.reduce_window(
            power_spec, zero_init, lax.add, (1, 2 * SMOOTH + 1), (1, 1), [(0, 0), (SMOOTH, SMOOTH)]
        )
        / counts
    )
    inv_scale = 1.0 / jnp.sqrt(smoothed + 1e-06)
    return jnp.concatenate([spec_re * inv_scale, spec_im * inv_scale], axis=1)


def cut_segments(extended):
    return jnp.stack([extended], axis=0)


def correlate(src_spec, recv_spec, src_valid, recv_valid, inv_tab):
    src_re = src_spec[:, None, :NF]
    src_im = src_spec[:, None, NF:]
    rec_re = recv_spec[None, :, :NF]
    rec_im = recv_spec[None, :, NF:]
    cross_re = src_re * rec_re + src_im * rec_im
    cross_im = src_re * rec_im - src_im * rec_re
    src_count = src_spec.shape[0]
    row_count = recv_spec.shape[0]
    cross = jnp.concatenate([cross_re, cross_im], axis=2).reshape(src_count * row_count, 2 * NF)
    lag_corr = jnp.dot(
        cross, inv_tab, precision=lax.Precision.HIGHEST, preferred_element_type=jnp.float32
    )
    lag_corr = lag_corr.reshape(src_count, row_count, LAGS)
    normed = lag_corr / jnp.sqrt(jnp.mean(lag_corr * lag_corr, axis=2, keepdims=True) + 1e-06)
    return normed * (src_valid[:, None] * recv_valid[None, :])[:, :, None]


def local(record, source_channels, valid_mask):
    row_count = record.shape[0]
    seg_count = valid_mask.shape[1]
    inv_tab = inverse_table()
    following = shifted(record, "tm", -1)
    extended = jnp.concatenate([record, following], axis=1)
    local_segments = cut_segments(extended).reshape(seg_count * row_count, SEGLEN)
    local_spec = whiten(local_segments).reshape(seg_count, row_count, 2 * NF)
    recv_mask = valid_mask.astype(jnp.float32).T
    first_row = lax.axis_index("recv") * row_count
    row_ids = lax.broadcasted_iota(jnp.int32, (NSRC, row_count), 1) + first_row
    onehot = (source_channels[:, None] == row_ids).astype(jnp.float32)
    picked_mask = jnp.dot(
        recv_mask, onehot.T, precision=lax.Precision.HIGHEST, preferred_element_type=jnp.float32
    )
    picked = jnp.einsum("sr,krc->ksc", onehot, local_spec, precision=lax.Precision.HIGHEST)
    src_spec, src_mask = lax.psum((picked, picked_mask), "recv")
    partial_stack = correlate(src_spec[0], local_spec[0], src_mask[0], recv_mask[0], inv_tab)
    lag_stack = lax.psum_scatter(partial_stack, "tm", scatter_dimension=0, tiled=True)
    return lag_stack


def solution(mesh):
    placed = (P("recv", "tm"), P(), P("recv", "tm"))
    return jax.shard_map(
        local, mesh=mesh, in_specs=placed, out_specs=P("tm", "recv", None), check_vma=False
    )
```

profile of v0, /device:TPU:1, one launch (start us, length us, event | category | flops | bytes accessed | tf_op | source)
XLA Modules:
  0.0 1716.2 jit_solution(3175187817627804121)
XLA Ops:
  6.5 0.0 all-reduce.2.cloned.1.call-start
  6.5 8.7 collective-permute-start
  15.3 0.1 sine_negate_fusion.3
  15.4 1.0 reduce_sum.29
  16.4 0.9 copy.6
  17.2 0.7 convert_bitcast_fusion
  17.9 0.9 convolution_bitcast_fusion.1
  18.7 325.6 %psum.15 = f32[16]{0:T(128)S(1)} all-reduce(f32[16]{0:T(128)S(1)} %convolution_bitcast_fusion.1), channel_id=1, replica_groups=mesh['recv'=128,'tm'=4] {'recv'}, use_global_device_ids=true, to_apply=%region_5.6 | all-reduce | flops 16 | bytes 128 | tf_op jit(solution)/shard_map/psum | solution.py:126
  344.3 4.2 cosine_multiply_fusion
  348.5 0.1 multiply_subtract_fusion.4
  348.6 0.0 collective-permute-done
  348.6 0.1 reduce_sum.30
  348.7 0.3 fusion.21
  349.1 0.3 fusion.23
  349.4 0.4 fusion.19
  349.8 0.4 fusion.17
  350.2 0.4 fusion.7
  350.6 0.2 copy.4
  350.8 0.3 reshape.179
  351.1 0.0 copy-start
  351.1 0.4 fusion.6
  351.5 0.0 copy-start.1
  351.5 0.2 copy.5
  351.7 0.3 reshape.180
  352.0 16.6 reduce_window.6
  368.6 0.0 copy-done
  368.6 0.0 copy-done.1
  368.6 1.1 convolution_bitcast_fusion
  369.7 0.0 all-reduce.2.cloned.1.call-update
  369.7 0.0 reduce-scatter.2.cloned.1.call-start
  369.8 0.1 broadcast_multiply_fusion
  369.9 1288.5 %all-reduce.2.cloned.1.call-done = f32[16,2048]{1,0:T(8,128)} async-done(((f32[16,2048]{1,0:T(8,128)}), f32[16,2048]{1,0:T(8,128)}) %all-reduce.2.cloned.1.call-update) | async-done | bytes 131088 | tf_op jit(solution)/shard_map/psum | solution.py:126
  1658.4 0.9 fusion.103
  1659.2 0.3 multiply_add_fusion
  1659.5 2.0 multiply_reduce_fusion
  1661.5 0.8 divide_multiply_fusion
  1662.4 0.0 reduce-scatter.2.cloned.1.call-update
  1662.4 46.9 %reduce-scatter.2.cloned.1.call-done = f32[4,16,256]{2,1,0:T(8,128)} async-done(((f32[16,16,256]{2,1,0:T(8,128)}), f32[4,16,256]{2,1,0:T(8,128)}) %reduce-scatter.2.cloned.1.call-update) | async-done | bytes 65552 | tf_op jit(solution)/shard_map/reduce_scatter | solution.py:128
  (9 shorter events, 0.1 us)
Async XLA Ops:
  6.5 1651.8 %all-reduce.2.cloned.1.call-start = ((), (), s32[]{:S(2)}) async-start(), calls=%async_computation.1 | async-start | bytes 262144 | tf_op jit(solution)/shard_map/psum | solution.py:126
  6.5 342.0 %collective-permute-start = (f32[16,1024]{1,0:T(8,128)}, f32[16,1024]{1,0:T(8,128)S(1)}, u32[]{:S(2)}, u32[]{:S(2)}) collective-permute-start(f32[16,1024]{1,0:T(8,128)} %param.3), channel_id=1, source_target_pairs={{1,0},{2,1},{3,2},{5,4},{6,5},{7,6},{9,8},{10,9},{11,10},{13,12},{... | collective-permute-start | bytes 196616 | tf_op jit(solution)/shard_map/ppermute | solution.py:16
  351.1 17.5 %copy-start = (f32[1024]{0:T(1024)S(1)}, f32[1024]{0:T(1024)}, u32[]{:S(2)}) copy-start(f32[1024]{0:T(1024)} %constant.98.clone.1) | copy-start | bytes 12292
  351.5 17.1 copy-start.1
  369.7 1339.6 %reduce-scatter.2.cloned.1.call-start = ((), (), s32[]{:S(2)}) async-start(), calls=%async_computation.2 | async-start | bytes 327680 | tf_op jit(solution)/shard_map/reduce_scatter | solution.py:128
Sparse Core Ops, SparseCore 0:
  369.9 1288.4 all-reduce.1
  1662.5 46.7 reduce-scatter.1
where the time goes:
time: 1720 us
  waiting for transfers between devices  1340 us (78%)
  blocking collectives  326 us (19%)
  other arithmetic  23.9 us (1%)
    psum x1, waiting for transfers between devices, local(): src_spec, src_mask = lax.psum((picked, picked_mask), 'recv')  1290 us
    psum x1, blocking collectives, local(): src_spec, src_mask = lax.psum((picked, picked_mask), 'recv')  326 us
    reduce_scatter x1, waiting for transfers between devices, local(): lax.psum_scatter(partial_stack, 'tm', scatter_dimension=0, tiled=True)  46.9 us
  transfers between devices with their start and end apart: 3, of which 2 were waited for; matrix products, arithmetic and copies ran while one was open for 0% of the time, Pallas kernels for 0%

commit v1 on v0

v1 whole, which is shorter than its diff:
```python
import functools

import jax
import jax.numpy as jnp
import numpy as np
from jax import lax
from jax.experimental import pallas as pl
from jax.experimental.pallas import tpu as pltpu
from jax.sharding import PartitionSpec as P

SEGLEN = 2048
NF = 1024
LAGS = 256
SMOOTH = 64
NSRC = 16
SEGS = 4
ROWS = 16
HALF = 1024
LANES = 128
OWNERS = 8
PLANES = 8
COLS = 4
MINE = 4
MESH = pl.DeviceIdType.MESH


def split_bf16(table):
    bf16 = jnp.dtype(jnp.bfloat16)
    high = table.astype(bf16)
    low = (table - high.astype(np.float64)).astype(bf16)
    return high, low


@functools.cache
def tables():
    m = np.arange(16)[:, None]
    lane = np.arange(LANES)[None, :]
    taper = 0.5 - 0.5 * np.cos(2 * np.pi * (m * 128 + lane) / SEGLEN)
    twist = 2 * np.pi * m * lane / SEGLEN
    j = np.arange(8)[:, None]
    freq = j + 8 * (lane // 64) + 16 * (lane % 64)
    counts = np.minimum(freq + SMOOTH, NF - 1) - np.maximum(freq - SMOOTH, 0) + 1
    small = np.concatenate([taper, np.cos(twist), np.sin(twist), 1.0 / counts]).astype(np.float32)

    angle = 2 * np.pi * (np.arange(128)[:, None] * np.arange(64)[None, :] % 128) / 128
    forward = np.zeros((4, 128, 4, 64))
    for h in range(2):
        forward[2 * h, :, h] = np.cos(angle)
        forward[2 * h + 1, :, h] = np.sin(angle)
        forward[2 * h, :, 2 + h] = -np.sin(angle)
        forward[2 * h + 1, :, 2 + h] = np.cos(angle)
    forward = forward.reshape(512, 256)

    lag = np.arange(LAGS)[None, None, :] - LAGS // 2
    turn = 2 * np.pi * (freq[:, :, None] * lag % SEGLEN) / SEGLEN
    factor = np.where(freq == 0, 1.0, 2.0)[:, :, None] / SEGLEN
    inverse = np.stack([factor * np.cos(turn), -factor * np.sin(turn)], axis=1).reshape(2 * NF, LAGS)
    return small, np.stack(split_bf16(forward)), np.stack(split_bf16(inverse))


def halves(x):
    high = x.astype(jnp.bfloat16)
    low = (x - high.astype(jnp.float32)).astype(jnp.bfloat16)
    return high, low


def dot3(high, low, tab_high, tab_low):
    dot = functools.partial(jnp.dot, preferred_element_type=jnp.float32)
    return dot(high, tab_high) + dot(low, tab_high) + dot(high, tab_low)


def real_dft16(x):
    r2 = np.float32(np.sqrt(0.5))
    c1 = np.float32(np.cos(np.pi / 8))
    s1 = np.float32(np.sin(np.pi / 8))
    a = [x[m] + x[m + 8] for m in range(8)]
    b = [x[m] - x[m + 8] for m in range(8)]
    a2 = [a[m] + a[m + 4] for m in range(4)]
    b2 = [a[m] - a[m + 4] for m in range(4)]
    even, odd = a2[0] + a2[2], a2[1] + a2[3]
    out = [None] * 9
    out[0] = (even + odd, None)
    out[8] = (even - odd, None)
    out[4] = (a2[0] - a2[2], a2[3] - a2[1])
    diff, total = r2 * (b2[1] - b2[3]), r2 * (b2[1] + b2[3])
    out[2] = (b2[0] + diff, -(b2[2] + total))
    out[6] = (b2[0] - diff, b2[2] - total)
    u1, u2, u3 = b[1] - b[7], r2 * (b[2] - b[6]), b[3] - b[5]
    v1, v2, v3 = b[1] + b[7], r2 * (b[2] + b[6]), b[3] + b[5]
    up, um = b[0] + u2, b[0] - u2
    vp, vm = v2 + b[4], v2 - b[4]
    p, q = c1 * u1 + s1 * u3, s1 * u1 - c1 * u3
    out[1] = (up + p, -(s1 * v1 + c1 * v3 + vp))
    out[7] = (up - p, -(s1 * v1 + c1 * v3 - vp))
    out[3] = (um + q, -(c1 * v1 - s1 * v3 + vm))
    out[5] = (um - q, -(c1 * v1 - s1 * v3 - vm))
    return out


def whitened(x, small, forward):
    total = x[0]
    for m in range(1, 16):
        total = total + x[m]
    mean = jnp.sum(total, axis=1, keepdims=True) * (1.0 / SEGLEN)
    tapered = [(x[m] - mean) * small[m : m + 1, :] for m in range(16)]
    base = real_dft16(tapered)
    mid = []
    for f in range(16):
        re, im = base[min(f, 16 - f)]
        if im is not None and f > 8:
            im = -im
        cos, sin = small[16 + f : 17 + f, :], small[32 + f : 33 + f, :]
        if f == 0:
            mid.append((re, jnp.zeros_like(re)))
        elif im is None:
            mid.append((re * cos, -(re * sin)))
        else:
            mid.append((re * cos + im * sin, im * cos - re * sin))
    highs, lows = [], []
    for j in range(8):
        parts = [halves(v) for v in (*mid[j], *mid[j + 8])]
        highs.append(jnp.concatenate([p[0] for p in parts], axis=1))
        lows.append(jnp.concatenate([p[1] for p in parts], axis=1))
    spec = dot3(jnp.concatenate(highs, axis=0), jnp.concatenate(lows, axis=0), forward[0], forward[1])
    rows = x[0].shape[0]
    re = [spec[j * rows : (j + 1) * rows, :LANES] for j in range(8)]
    im = [spec[j * rows : (j + 1) * rows, LANES:] for j in range(8)]
    power = [re[j] * re[j] + im[j] * im[j] for j in range(8)]

    lane = lax.broadcasted_iota(jnp.int32, power[0].shape, 1)
    bin_g = lane % 64
    lower = lane < 64
    zero = jnp.zeros_like(power[0])
    ahead, behind = [power[0]], [power[7]]
    for j in range(1, 8):
        ahead.append(ahead[-1] + power[j])
        behind.append(behind[-1] + power[7 - j])
    behind.reverse()
    other = pltpu.roll(ahead[7], 64, 1)
    lower_total = jnp.where(lower, zero, other)
    upper_total = jnp.where(lower, other, zero)
    all_f = jnp.where(lower, ahead[7] + other, zero)
    three = all_f + pltpu.roll(all_f, 1, 1) + pltpu.roll(all_f, 2, 1)
    seven = jnp.where(lower, pltpu.roll(three, 125, 1) + all_f + pltpu.roll(three, 1, 1), zero)
    seven = seven + pltpu.roll(seven, 64, 1)
    out_re, out_im = [], []
    for j in range(8):
        above = jnp.where(bin_g < 60, pltpu.roll(ahead[j] + lower_total, 124, 1), zero)
        below = jnp.where(bin_g >= 4, pltpu.roll(behind[j] + upper_total, 4, 1), zero)
        smoothed = (seven + above + below) * small[48 + j : 49 + j, :]
        scale = lax.rsqrt(smoothed + 1e-06)
        out_re.append(re[j] * scale)
        out_im.append(im[j] * scale)
    return out_re, out_im


def kernel(
    chan_ref, mask_ref, rec_ref, small_ref, fwd_hbm, inv_hbm, out_ref,
    fwd_ref, inv_ref, all_ref, val_ref, vsend_ref, send1_ref, recv1_ref, send2_ref, recv2_ref,
    white_ref, src_ref, high_ref, low_ref,
    tab_sem, rec_ssem, rec_rsem, val_ssem, val_rsem, ssem1, rsem1, ssem2, rsem2,
):
    r = lax.axis_index("recv")
    t = lax.axis_index("tm")
    x, yh, z = r % COLS, (r // COLS) % 4, r // 16
    cand = r % OWNERS
    group = r // OWNERS
    dest = z // 2

    load_fwd = pltpu.make_async_copy(fwd_hbm, fwd_ref, tab_sem.at[0])
    load_inv = pltpu.make_async_copy(inv_hbm, inv_ref, tab_sem.at[1])
    load_fwd.start()
    load_inv.start()

    barrier = pltpu.get_barrier_semaphore()

    def greet(recv, tm):
        pl.semaphore_signal(barrier, inc=1, device_id={"recv": recv, "tm": tm}, device_id_type=MESH)

    for d in range(1, OWNERS):
        greet(group * OWNERS + (cand + d) % OWNERS, t)
    for d in range(1, SEGS):
        greet(r, (t + d) % SEGS)
    for p in range(2):
        for b in range(SEGS):
            for flip in range(2):
                plane = 2 * t + p
                row = yh if flip == 0 else 3 - yh
                if flip == 0:

                    @pl.when(jnp.logical_or(plane != z, t != b))
                    def _(plane=plane, row=row, b=b):
                        greet(plane * 16 + row * COLS + x, b)
                else:
                    greet(plane * 16 + row * COLS + x, b)

    rec = rec_ref[...]
    valid = jnp.broadcast_to(mask_ref[...].astype(jnp.float32), (ROWS, LANES))
    vsend_ref[...] = valid
    val_ref[t] = valid
    all_ref[t] = rec
    all_ref[SEGS] = jnp.zeros((ROWS, HALF), jnp.float32)

    index = jnp.clip(chan_ref[group] - r * ROWS, 0, ROWS - 1)
    picked = rec_ref[pl.ds(index, 1), :]
    for m in range(8):
        piece = picked[:, m * LANES : (m + 1) * LANES]
        send1_ref[pl.ds(m, 1), :] = piece
        recv1_ref[cand, pl.ds(m, 1), :] = piece
    piece = vsend_ref[pl.ds(index, 1), :]
    send1_ref[pl.ds(8, 1), :] = piece
    recv1_ref[cand, pl.ds(8, 1), :] = piece

    is_self = (t == dest).astype(jnp.int32)
    pl.semaphore_wait(barrier, (OWNERS - 1) + (SEGS - 1) + 16 - is_self)

    sends = []
    for d in range(1, OWNERS):
        copy = pltpu.make_async_remote_copy(
            send1_ref, recv1_ref.at[cand], ssem1.at[d], rsem1.at[cand],
            device_id={"recv": group * OWNERS + (cand + d) % OWNERS, "tm": t}, device_id_type=MESH,
        )
        copy.start()
        sends.append(copy)
    for d in range(1, SEGS):
        to = {"recv": r, "tm": (t + d) % SEGS}
        copy = pltpu.make_async_remote_copy(
            rec_ref, all_ref.at[t], rec_ssem.at[d], rec_rsem.at[t], device_id=to, device_id_type=MESH
        )
        copy.start()
        sends.append(copy)
        copy = pltpu.make_async_remote_copy(
            vsend_ref, val_ref.at[t], val_ssem.at[d], val_rsem.at[t], device_id=to, device_id_type=MESH
        )
        copy.start()
        sends.append(copy)

    def arrived(buf, sem):
        pltpu.make_async_remote_copy(
            buf, buf, sem, sem, device_id={"recv": r, "tm": t}, device_id_type=MESH
        ).wait_recv()

    for d in range(1, OWNERS):
        slot = (cand + d) % OWNERS
        arrived(recv1_ref.at[slot], rsem1.at[slot])

    owner = jnp.clip((chan_ref[group] - group * (OWNERS * ROWS)) // ROWS, 0, OWNERS - 1)
    chosen = recv1_ref[owner]
    send2_ref[...] = chosen
    entry = t * MINE + (z % 2) * 2 + yh // 2

    @pl.when(t == dest)
    def _():
        recv2_ref[entry] = chosen

    sends2 = []
    for n, dz in enumerate((4, 3, 5, 2, 6, 1, 7, 0)):
        for flip in range(2):
            row = yh if flip == 0 else 3 - yh
            copy = pltpu.make_async_remote_copy(
                send2_ref, recv2_ref.at[entry], ssem2.at[2 * n + flip], rsem2.at[entry],
                device_id={"recv": ((z + dz) % PLANES) * 16 + row * COLS + x, "tm": dest},
                device_id_type=MESH,
            )
            if dz == 0 and flip == 0:
                pl.when(t != dest)(copy.start)
            else:
                copy.start()
                sends.append(copy)
            sends2.append(copy)

    for d in range(1, SEGS):
        slot = (t + d) % SEGS
        arrived(all_ref.at[slot], rec_rsem.at[slot])
        arrived(val_ref.at[slot], val_rsem.at[slot])
    load_fwd.wait()
    small = small_ref[...]

    @pl.loop(0, SEGS)
    def _(k):
        first, second = all_ref[k], all_ref[k + 1]
        xs = [first[:, m * LANES : (m + 1) * LANES] for m in range(8)]
        xs += [second[:, m * LANES : (m + 1) * LANES] for m in range(8)]
        re, im = whitened(xs, small, (fwd_ref[0], fwd_ref[1]))
        for j in range(8):
            white_ref[k, j, :, :LANES] = re[j]
            white_ref[k, j, :, LANES:] = im[j]

    for e in range(SEGS * MINE):
        b, p, h = e // MINE, (e % MINE) // 2, e % 2
        own = jnp.logical_and(jnp.logical_and(t == b, z == 2 * t + p), yh // 2 == h)

        @pl.when(jnp.logical_not(own))
        def _(e=e):
            arrived(recv2_ref.at[e], rsem2.at[e])

    none = jnp.zeros((MINE, LANES), jnp.float32)
    xs = [recv2_ref[:, m, :] for m in range(8)]
    xs += [jnp.concatenate([v[MINE:], none], axis=0) for v in xs]
    re, im = whitened(xs, small, (fwd_ref[0], fwd_ref[1]))
    for j in range(8):
        src_ref[j, :, :LANES] = re[j]
        src_ref[j, :, LANES:] = im[j]

    @pl.loop(0, SEGS)
    def _(k):
        for j in range(8):
            rec_re, rec_im = white_ref[k, j, :, :LANES], white_ref[k, j, :, LANES:]
            for s in range(MINE):
                src = src_ref[j, pl.ds(k * MINE + s, 1), :]
                src_re, src_im = src[:, :LANES], src[:, LANES:]
                cross_re = src_re * rec_re + src_im * rec_im
                cross_im = src_re * rec_im - src_im * rec_re
                rows = pl.ds(pl.multiple_of(k * (MINE * ROWS), MINE * ROWS) + s * ROWS, ROWS)
                for part, value in enumerate((cross_re, cross_im)):
                    high, low = halves(value)
                    first = (2 * j + part) * LANES
                    high_ref[rows, first : first + LANES] = high
                    low_ref[rows, first : first + LANES] = low

    load_inv.wait()
    lag = dot3(high_ref[...], low_ref[...], inv_ref[0], inv_ref[1])
    power = jnp.sum(lag * lag, axis=1, keepdims=True) * (1.0 / LAGS)
    scale = lax.rsqrt(power + 1e-06)
    for s in range(MINE):
        stack = None
        for k in range(SEGS):
            first = (k * MINE + s) * ROWS
            weight = val_ref[k] * recv2_ref[k * MINE + s, pl.ds(8, 1), :]
            term = lag[first : first + ROWS] * (scale[first : first + ROWS] * weight[:, :1])
            stack = term if stack is None else stack + term
        out_ref[s] = stack

    for copy in sends:
        copy.wait_send()

    @pl.when(t != dest)
    def _():
        sends2[14].wait_send()


def local(record, source_channels, valid_mask):
    small, forward, inverse = tables()
    f32, bf16 = jnp.float32, jnp.bfloat16
    vmem = pl.BlockSpec(memory_space=pltpu.VMEM)
    hbm = pl.BlockSpec(memory_space=pltpu.HBM)
    dma = pltpu.SemaphoreType.DMA
    return pl.pallas_call(
        kernel,
        out_shape=jax.ShapeDtypeStruct((MINE, ROWS, LAGS), f32),
        in_specs=[pl.BlockSpec(memory_space=pltpu.SMEM), vmem, vmem, vmem, hbm, hbm],
        out_specs=vmem,
        scratch_shapes=[
            pltpu.VMEM((2, 512, 256), bf16),
            pltpu.VMEM((2, 2 * NF, LAGS), bf16),
            pltpu.VMEM((SEGS + 1, ROWS, HALF), f32),
            pltpu.VMEM((SEGS, ROWS, LANES), f32),
            pltpu.VMEM((ROWS, LANES), f32),
            pltpu.VMEM((9, LANES), f32),
            pltpu.VMEM((OWNERS, 9, LANES), f32),
            pltpu.VMEM((9, LANES), f32),
            pltpu.VMEM((SEGS * MINE, 9, LANES), f32),
            pltpu.VMEM((SEGS, 8, ROWS, 256), f32),
            pltpu.VMEM((8, SEGS * MINE, 256), f32),
            pltpu.VMEM((SEGS * MINE * ROWS, 2 * NF), bf16),
            pltpu.VMEM((SEGS * MINE * ROWS, 2 * NF), bf16),
            dma((2,)), dma((SEGS,)), dma((SEGS,)), dma((SEGS,)), dma((SEGS,)),
            dma((OWNERS,)), dma((OWNERS,)), dma((16,)), dma((16,)),
        ],
        compiler_params=pltpu.CompilerParams(
            collective_id=0, has_side_effects=True, vmem_limit_bytes=60 * 2**20
        ),
        name="correlate",
    )(source_channels, valid_mask, record, jnp.asarray(small), jnp.asarray(forward), jnp.asarray(inverse))


def solution(mesh):
    placed = (P("recv", "tm"), P(), P("recv", "tm"))
    return jax.shard_map(
        local, mesh=mesh, in_specs=placed, out_specs=P("tm", "recv", None), check_vma=False
    )
```

time: 1720 us -> 33.4 us (0.02)
  waiting for transfers between devices: 1340 us -> 0 us
  blocking collectives: 326 us -> 0 us
  Pallas kernels: 0 us -> 30.3 us
  other arithmetic: 23.9 us -> 0 us
    psum x1 -> x0, waiting for transfers between devices: 1290 us -> none  [local(): src_spec, src_mask = lax.psum((picked, picked_mask), 'recv')]
    psum x1 -> x0, blocking collectives: 326 us -> none  [local(): src_spec, src_mask = lax.psum((picked, picked_mask), 'recv')]
    reduce_scatter x1 -> x0, waiting for transfers between devices: 46.9 us -> none  [local(): lax.psum_scatter(partial_stack, 'tm', scatter_dimension=0, tiled=True)]
    pallas_call x0 -> x1, Pallas kernels: none -> 30.3 us  [local(): pl.pallas_call(kernel, out_shape=jax.ShapeDtypeStruct((MINE, ROWS, LAGS),...]
    another operation x2 -> x0, other arithmetic: 17.2 us -> none  [the longest x1 16.6 us: whiten(): lax.reduce_window(power_spec, zero_init, lax.add, (1, 2 * SMOOTH + 1), (1...]
  transfers between devices with their start and end apart: 3 -> 0, of which waited for: 2 -> 0; matrix products, arithmetic and copies ran while one was open for 0% -> 0% of each run, Pallas kernels for 0% -> 0%
where the time goes in v1:
time: 33.4 us; the launch traced here: 33.1 us
  Pallas kernels  30.3 us (91%)
  local copies, waits for them, and re-layouts  2.8 us (8%)
    pallas_call x1, Pallas kernels, local(): pl.pallas_call(kernel, out_shape=jax.ShapeDtypeStruct((MINE, ROWS, LAGS),...  30.3 us
    unnamed x2, local copies, waits for them, and re-layouts  2.8 us

profile of v1, /device:TPU:1, one launch (start us, length us, event | category | flops | bytes accessed | tf_op | source)
XLA Modules:
  0.0 33.1 jit_solution(15942239233564841526)
XLA Ops:
  0.0 1.3 %copy.7.mask_ref = s32[16,1]{1,0:T(8,128)} copy(s32[16,1]{0,1:T(1,128)} %param.8) | data formatting | bytes 128 | tf_op args[2]
  1.3 30.3 %correlate.1 = f32[4,16,256]{2,1,0:T(8,128)} custom-call(s32[16]{0:T(128)} %chan_ref.1, s32[16,1]{1,0:T(8,128)} %copy.7.mask_ref, f32[16,1024]{1,0:T(8,128)} %rec_ref.1, f32[56,128]{1,0:T(8,128)} %constant.6.clone.small_ref, bf16[2,512,256]{2,1,0:T(8,128)(2,1)} %constant.7.clone.fwd_hbm, bf16[2,2048,256]{2,1,0:T(8,128)(2,1)} %constant.8.clone.inv_hbm), custom_call_target="tpu_custom_call" | custom-call | tf_op jit(solution)/shard_map/correlate/pallas_call | solution.py:348
  31.7 1.5 %copy.9 = f32[4,16,256]{2,1,0:T(8,128)} copy(f32[4,16,256]{2,1,0:T(8,128)} %correlate.1) | data formatting | bytes 131072

commit v2 on v1

--- a/solution.py
+++ b/solution.py
@@ -158,7 +158,7 @@
     chan_ref, mask_ref, rec_ref, small_ref, fwd_hbm, inv_hbm, out_ref,
     fwd_ref, inv_ref, all_ref, val_ref, vsend_ref, send1_ref, recv1_ref, send2_ref, recv2_ref,
     white_ref, src_ref, high_ref, low_ref,
-    tab_sem, rec_ssem, rec_rsem, val_ssem, val_rsem, ssem1, rsem1, ssem2, rsem2,
+    tab_sem, rec_ssem, rec_rsem, val_ssem, val_rsem, ssem1, rsem1, ssem2, rsem2, ready_sem,
 ):
     r = lax.axis_index("recv")
     t = lax.axis_index("tm")
@@ -177,25 +177,38 @@
     def greet(recv, tm):
         pl.semaphore_signal(barrier, inc=1, device_id={"recv": recv, "tm": tm}, device_id_type=MESH)
 
+    rows = (yh, 3 - yh)
     for d in range(1, OWNERS):
         greet(group * OWNERS + (cand + d) % OWNERS, t)
     for d in range(1, SEGS):
         greet(r, (t + d) % SEGS)
+
+    @pl.when(t == dest)
+    def _():
+        for b in range(SEGS):
+            greet(z * 16 + rows[1] * COLS + x, b)
+
     for p in range(2):
-        for b in range(SEGS):
-            for flip in range(2):
-                plane = 2 * t + p
-                row = yh if flip == 0 else 3 - yh
-                if flip == 0:
-
-                    @pl.when(jnp.logical_or(plane != z, t != b))
-                    def _(plane=plane, row=row, b=b):
-                        greet(plane * 16 + row * COLS + x, b)
-                else:
-                    greet(plane * 16 + row * COLS + x, b)
+
+        @pl.when(2 * t + p > z)
+        def _(p=p):
+            for b in range(SEGS):
+                for row in rows:
+                    greet((2 * t + p) * 16 + row * COLS + x, b)
+
+    for target in range(1, PLANES):
+
+        @pl.when(target > z)
+        def _(target=target):
+            for row in rows:
+                greet(target * 16 + row * COLS + x, dest)
 
     rec = rec_ref[...]
-    valid = jnp.broadcast_to(mask_ref[...].astype(jnp.float32), (ROWS, LANES))
+    mask = jnp.broadcast_to(mask_ref[...].astype(jnp.float32), (ROWS, ROWS))
+    square = (ROWS, ROWS)
+    diagonal = lax.broadcasted_iota(jnp.int32, square, 0) == lax.broadcasted_iota(jnp.int32, square, 1)
+    mask = jnp.sum(jnp.where(diagonal, mask, 0.0), axis=1, keepdims=True)
+    valid = jnp.broadcast_to(mask, (ROWS, LANES))
     vsend_ref[...] = valid
     val_ref[t] = valid
     all_ref[t] = rec
@@ -211,8 +224,19 @@
     send1_ref[pl.ds(8, 1), :] = piece
     recv1_ref[cand, pl.ds(8, 1), :] = piece
 
-    is_self = (t == dest).astype(jnp.int32)
-    pl.semaphore_wait(barrier, (OWNERS - 1) + (SEGS - 1) + 16 - is_self)
+    lower_holders = jnp.clip(z - 2 * t, 0, 2)
+    pl.semaphore_wait(barrier, (OWNERS - 1) + (SEGS - 1) + 1 + 2 * z + 8 * lower_holders)
+
+    for p in range(2):
+
+        @pl.when(2 * t + p < z)
+        def _(p=p):
+            for b in range(SEGS):
+                for flip, row in enumerate(rows):
+                    pl.semaphore_signal(
+                        ready_sem.at[2 * z + flip], inc=1,
+                        device_id={"recv": (2 * t + p) * 16 + row * COLS + x, "tm": b}, device_id_type=MESH,
+                    )
 
     sends = []
     for d in range(1, OWNERS):
@@ -253,21 +277,15 @@
     def _():
         recv2_ref[entry] = chosen
 
-    sends2 = []
-    for n, dz in enumerate((4, 3, 5, 2, 6, 1, 7, 0)):
-        for flip in range(2):
-            row = yh if flip == 0 else 3 - yh
-            copy = pltpu.make_async_remote_copy(
-                send2_ref, recv2_ref.at[entry], ssem2.at[2 * n + flip], rsem2.at[entry],
-                device_id={"recv": ((z + dz) % PLANES) * 16 + row * COLS + x, "tm": dest},
-                device_id_type=MESH,
-            )
-            if dz == 0 and flip == 0:
-                pl.when(t != dest)(copy.start)
-            else:
-                copy.start()
-                sends.append(copy)
-            sends2.append(copy)
+    def spread(target, flip):
+        return pltpu.make_async_remote_copy(
+            send2_ref, recv2_ref.at[entry], ssem2.at[2 * target + flip], rsem2.at[entry],
+            device_id={"recv": target * 16 + rows[flip] * COLS + x, "tm": dest}, device_id_type=MESH,
+        )
+
+    for target in range(PLANES):
+        pl.when(target <= z)(spread(target, 1).start)
+        pl.when(jnp.logical_or(target < z, jnp.logical_and(target == z, t != dest)))(spread(target, 0).start)
 
     for d in range(1, SEGS):
         slot = (t + d) % SEGS
@@ -285,6 +303,14 @@
         for j in range(8):
             white_ref[k, j, :, :LANES] = re[j]
             white_ref[k, j, :, LANES:] = im[j]
+
+    for target in range(1, PLANES):
+
+        @pl.when(target > z)
+        def _(target=target):
+            for flip in range(2):
+                pl.semaphore_wait(ready_sem.at[2 * target + flip], 1)
+                spread(target, flip).start()
 
     for e in range(SEGS * MINE):
         b, p, h = e // MINE, (e % MINE) // 2, e % 2
@@ -334,9 +360,9 @@
     for copy in sends:
         copy.wait_send()
 
-    @pl.when(t != dest)
-    def _():
-        sends2[14].wait_send()
+    for target in range(PLANES):
+        spread(target, 1).wait_send()
+        pl.when(jnp.logical_or(target != z, t != dest))(spread(target, 0).wait_send)
 
 
 def local(record, source_channels, valid_mask):
@@ -365,13 +391,13 @@
             pltpu.VMEM((SEGS * MINE * ROWS, 2 * NF), bf16),
             pltpu.VMEM((SEGS * MINE * ROWS, 2 * NF), bf16),
             dma((2,)), dma((SEGS,)), dma((SEGS,)), dma((SEGS,)), dma((SEGS,)),
-            dma((OWNERS,)), dma((OWNERS,)), dma((16,)), dma((16,)),
+            dma((OWNERS,)), dma((OWNERS,)), dma((16,)), dma((16,)), pltpu.SemaphoreType.REGULAR((16,)),
         ],
         compiler_params=pltpu.CompilerParams(
             collective_id=0, has_side_effects=True, vmem_limit_bytes=60 * 2**20
         ),
         name="correlate",
-    )(source_channels, valid_mask, record, jnp.asarray(small), jnp.asarray(forward), jnp.asarray(inverse))
+    )(source_channels, valid_mask.reshape(1, ROWS), record, jnp.asarray(small), jnp.asarray(forward), jnp.asarray(inverse))
 
 
 def solution(mesh):

time: 33.4 us -> 29.6 us (0.89)
  the two profiles are of different devices: /device:TPU:1 before, /device:TPU:9 now
where the time goes in v2:
time: 29.6 us; the launch traced here: 29.4 us
  Pallas kernels  27.9 us (94%)
  local copies, waits for them, and re-layouts  1.47 us (5%)
    pallas_call x1, Pallas kernels, local(): pl.pallas_call(kernel, out_shape=jax.ShapeDtypeStruct((MINE, ROWS, LAGS),...  27.9 us
    unnamed x1, local copies, waits for them, and re-layouts  1.47 us

profile of v2, /device:TPU:9, one launch (start us, length us, event | category | flops | bytes accessed | tf_op | source)
XLA Modules:
  0.0 29.4 jit_solution(2304257298617756767)
XLA Ops:
  0.0 27.9 %correlate.1 = f32[4,16,256]{2,1,0:T(8,128)} custom-call(s32[16]{0:T(128)} %chan_ref.1, s32[1,16]{1,0:T(1,128)} %bitcast.1, f32[16,1024]{1,0:T(8,128)} %rec_ref.1, f32[56,128]{1,0:T(8,128)} %constant.6.clone.small_ref, bf16[2,512,256]{2,1,0:T(8,128)(2,1)} %constant.7.clone.fwd_hbm, bf16[2,2048,256]{2,1,0:T(8,128)(2,1)} %constant.8.clone.inv_hbm), custom_call_target="tpu_custom_call" | custom-call | tf_op jit(solution)/shard_map/correlate/pallas_call | solution.py:374
  27.9 1.5 %copy.8 = f32[4,16,256]{2,1,0:T(8,128)} copy(f32[4,16,256]{2,1,0:T(8,128)} %correlate.1) | data formatting | bytes 131072

commit v3 on v2

--- a/solution.py
+++ b/solution.py
@@ -20,6 +20,7 @@
 OWNERS = 8
 PLANES = 8
 COLS = 4
+YROWS = 4
 MINE = 4
 MESH = pl.DeviceIdType.MESH
 
@@ -155,55 +156,70 @@
 
 
 def kernel(
-    chan_ref, mask_ref, rec_ref, small_ref, fwd_hbm, inv_hbm, out_ref,
-    fwd_ref, inv_ref, all_ref, val_ref, vsend_ref, send1_ref, recv1_ref, send2_ref, recv2_ref,
+    chan_hbm, mask_hbm, rec_hbm, small_hbm, fwd_hbm, inv_hbm, out_ref,
+    chan_ref, mask_ref, rec_ref, small_ref, fwd_ref, inv_ref,
+    all_ref, val_ref, vsend_ref, send1_ref, recv1_ref, send2_ref, recv2_ref,
     white_ref, src_ref, high_ref, low_ref,
     tab_sem, rec_ssem, rec_rsem, val_ssem, val_rsem, ssem1, rsem1, ssem2, rsem2, ready_sem,
 ):
     r = lax.axis_index("recv")
     t = lax.axis_index("tm")
-    x, yh, z = r % COLS, (r // COLS) % 4, r // 16
-    cand = r % OWNERS
-    group = r // OWNERS
+    x, yh, z = r % COLS, (r // COLS) % YROWS, r // 16
+    line = r - x
     dest = z // 2
 
-    load_fwd = pltpu.make_async_copy(fwd_hbm, fwd_ref, tab_sem.at[0])
-    load_inv = pltpu.make_async_copy(inv_hbm, inv_ref, tab_sem.at[1])
-    load_fwd.start()
-    load_inv.start()
+    loads = [
+        pltpu.make_async_copy(src, dst, tab_sem.at[n])
+        for n, (src, dst) in enumerate(
+            (
+                (rec_hbm, rec_ref),
+                (chan_hbm, chan_ref),
+                (mask_hbm, mask_ref),
+                (small_hbm, small_ref),
+                (fwd_hbm, fwd_ref),
+                (inv_hbm, inv_ref),
+            )
+        )
+    ]
+    for load in loads:
+        load.start()
 
     barrier = pltpu.get_barrier_semaphore()
+
+    def at(plane, row):
+        return plane * 16 + row * COLS + x
 
     def greet(recv, tm):
         pl.semaphore_signal(barrier, inc=1, device_id={"recv": recv, "tm": tm}, device_id_type=MESH)
 
-    rows = (yh, 3 - yh)
-    for d in range(1, OWNERS):
-        greet(group * OWNERS + (cand + d) % OWNERS, t)
+    for d in range(1, COLS):
+        greet(line + (x + d) % COLS, t)
     for d in range(1, SEGS):
         greet(r, (t + d) % SEGS)
 
     @pl.when(t == dest)
     def _():
         for b in range(SEGS):
-            greet(z * 16 + rows[1] * COLS + x, b)
+            for d in range(1, YROWS):
+                greet(at(z, (yh + d) % YROWS), b)
 
     for p in range(2):
 
         @pl.when(2 * t + p > z)
         def _(p=p):
             for b in range(SEGS):
-                for row in rows:
-                    greet((2 * t + p) * 16 + row * COLS + x, b)
+                for row in range(YROWS):
+                    greet(at(2 * t + p, row), b)
 
     for target in range(1, PLANES):
 
         @pl.when(target > z)
         def _(target=target):
-            for row in rows:
-                greet(target * 16 + row * COLS + x, dest)
-
-    rec = rec_ref[...]
+            for row in range(YROWS):
+                greet(at(target, row), dest)
+
+    for load in loads[:3]:
+        load.wait()
     mask = jnp.broadcast_to(mask_ref[...].astype(jnp.float32), (ROWS, ROWS))
     square = (ROWS, ROWS)
     diagonal = lax.broadcasted_iota(jnp.int32, square, 0) == lax.broadcasted_iota(jnp.int32, square, 1)
@@ -211,38 +227,31 @@
     valid = jnp.broadcast_to(mask, (ROWS, LANES))
     vsend_ref[...] = valid
     val_ref[t] = valid
-    all_ref[t] = rec
-    all_ref[SEGS] = jnp.zeros((ROWS, HALF), jnp.float32)
-
-    index = jnp.clip(chan_ref[group] - r * ROWS, 0, ROWS - 1)
+
+    def owner(source):
+        return jnp.clip((chan_ref[source] - source * (OWNERS * ROWS)) // ROWS, 0, OWNERS - 1)
+
+    source = r // OWNERS
+    index = jnp.clip(chan_ref[source] - r * ROWS, 0, ROWS - 1)
     picked = rec_ref[pl.ds(index, 1), :]
     for m in range(8):
         piece = picked[:, m * LANES : (m + 1) * LANES]
         send1_ref[pl.ds(m, 1), :] = piece
-        recv1_ref[cand, pl.ds(m, 1), :] = piece
+        recv1_ref[x, pl.ds(m, 1), :] = piece
     piece = vsend_ref[pl.ds(index, 1), :]
     send1_ref[pl.ds(8, 1), :] = piece
-    recv1_ref[cand, pl.ds(8, 1), :] = piece
+    recv1_ref[x, pl.ds(8, 1), :] = piece
+    all_ref[t] = rec_ref[...]
+    all_ref[SEGS] = jnp.zeros((ROWS, HALF), jnp.float32)
 
     lower_holders = jnp.clip(z - 2 * t, 0, 2)
-    pl.semaphore_wait(barrier, (OWNERS - 1) + (SEGS - 1) + 1 + 2 * z + 8 * lower_holders)
-
-    for p in range(2):
-
-        @pl.when(2 * t + p < z)
-        def _(p=p):
-            for b in range(SEGS):
-                for flip, row in enumerate(rows):
-                    pl.semaphore_signal(
-                        ready_sem.at[2 * z + flip], inc=1,
-                        device_id={"recv": (2 * t + p) * 16 + row * COLS + x, "tm": b}, device_id_type=MESH,
-                    )
+    pl.semaphore_wait(barrier, (COLS - 1) + (SEGS - 1) + (YROWS - 1) + YROWS * z + 16 * lower_holders)
 
     sends = []
-    for d in range(1, OWNERS):
+    for d in range(1, COLS):
         copy = pltpu.make_async_remote_copy(
-            send1_ref, recv1_ref.at[cand], ssem1.at[d], rsem1.at[cand],
-            device_id={"recv": group * OWNERS + (cand + d) % OWNERS, "tm": t}, device_id_type=MESH,
+            send1_ref, recv1_ref.at[x], ssem1.at[d], rsem1.at[x],
+            device_id={"recv": line + (x + d) % COLS, "tm": t}, device_id_type=MESH,
         )
         copy.start()
         sends.append(copy)
@@ -259,39 +268,54 @@
         copy.start()
         sends.append(copy)
 
+    for p in range(2):
+
+        @pl.when(2 * t + p < z)
+        def _(p=p):
+            for b in range(SEGS):
+                for row in range(YROWS):
+                    pl.semaphore_signal(
+                        ready_sem.at[YROWS * z + yh], inc=1,
+                        device_id={"recv": at(2 * t + p, row), "tm": b}, device_id_type=MESH,
+                    )
+
     def arrived(buf, sem):
         pltpu.make_async_remote_copy(
             buf, buf, sem, sem, device_id={"recv": r, "tm": t}, device_id_type=MESH
         ).wait_recv()
 
-    for d in range(1, OWNERS):
-        slot = (cand + d) % OWNERS
+    for d in range(1, COLS):
+        slot = (x + d) % COLS
         arrived(recv1_ref.at[slot], rsem1.at[slot])
 
-    owner = jnp.clip((chan_ref[group] - group * (OWNERS * ROWS)) // ROWS, 0, OWNERS - 1)
-    chosen = recv1_ref[owner]
+    chosen = recv1_ref[owner(source) % COLS]
     send2_ref[...] = chosen
     entry = t * MINE + (z % 2) * 2 + yh // 2
 
     @pl.when(t == dest)
     def _():
-        recv2_ref[entry] = chosen
-
-    def spread(target, flip):
+        recv2_ref[yh % 2, entry] = chosen
+
+    def spread(target, row):
+        n = YROWS * target + row
         return pltpu.make_async_remote_copy(
-            send2_ref, recv2_ref.at[entry], ssem2.at[2 * target + flip], rsem2.at[entry],
-            device_id={"recv": target * 16 + rows[flip] * COLS + x, "tm": dest}, device_id_type=MESH,
+            send2_ref, recv2_ref.at[yh % 2, entry], ssem2.at[n], rsem2.at[yh % 2, entry],
+            device_id={"recv": at(target, row), "tm": dest}, device_id_type=MESH,
         )
 
+    def apart(target, row):
+        return jnp.logical_or(jnp.logical_or(target != z, row != yh), t != dest)
+
     for target in range(PLANES):
-        pl.when(target <= z)(spread(target, 1).start)
-        pl.when(jnp.logical_or(target < z, jnp.logical_and(target == z, t != dest)))(spread(target, 0).start)
+        for row in range(YROWS):
+            pl.when(jnp.logical_and(target <= z, apart(target, row)))(spread(target, row).start)
 
     for d in range(1, SEGS):
         slot = (t + d) % SEGS
         arrived(all_ref.at[slot], rec_rsem.at[slot])
         arrived(val_ref.at[slot], val_rsem.at[slot])
-    load_fwd.wait()
+    loads[3].wait()
+    loads[4].wait()
     small = small_ref[...]
 
     @pl.loop(0, SEGS)
@@ -308,21 +332,31 @@
 
         @pl.when(target > z)
         def _(target=target):
-            for flip in range(2):
-                pl.semaphore_wait(ready_sem.at[2 * target + flip], 1)
-                spread(target, flip).start()
+            for row in range(YROWS):
+                pl.semaphore_wait(ready_sem.at[YROWS * target + row], 1)
+                spread(target, row).start()
 
     for e in range(SEGS * MINE):
-        b, p, h = e // MINE, (e % MINE) // 2, e % 2
-        own = jnp.logical_and(jnp.logical_and(t == b, z == 2 * t + p), yh // 2 == h)
-
-        @pl.when(jnp.logical_not(own))
-        def _(e=e):
-            arrived(recv2_ref.at[e], rsem2.at[e])
+        for half in range(2):
+            b, p, row = e // MINE, (e % MINE) // 2, 2 * (e % 2) + half
+            own = jnp.logical_and(jnp.logical_and(t == b, z == 2 * t + p), yh == row)
+
+            @pl.when(jnp.logical_not(own))
+            def _(e=e, half=half):
+                arrived(recv2_ref.at[half, e], rsem2.at[half, e])
+
+    turn = lax.broadcasted_iota(jnp.int32, (SEGS * MINE, LANES), 0) % MINE
+    upper = jnp.zeros((SEGS * MINE, LANES), jnp.int32)
+    for s in range(MINE):
+        upper = jnp.where(turn == s, owner(MINE * t + s) // COLS, upper)
+
+    def source_rows(m):
+        return jnp.where(upper == 1, recv2_ref[1, :, m, :], recv2_ref[0, :, m, :])
 
     none = jnp.zeros((MINE, LANES), jnp.float32)
-    xs = [recv2_ref[:, m, :] for m in range(8)]
+    xs = [source_rows(m) for m in range(8)]
     xs += [jnp.concatenate([v[MINE:], none], axis=0) for v in xs]
+    src_valid = source_rows(8)
     re, im = whitened(xs, small, (fwd_ref[0], fwd_ref[1]))
     for j in range(8):
         src_ref[j, :, :LANES] = re[j]
@@ -344,7 +378,7 @@
                     high_ref[rows, first : first + LANES] = high
                     low_ref[rows, first : first + LANES] = low
 
-    load_inv.wait()
+    loads[5].wait()
     lag = dot3(high_ref[...], low_ref[...], inv_ref[0], inv_ref[1])
     power = jnp.sum(lag * lag, axis=1, keepdims=True) * (1.0 / LAGS)
     scale = lax.rsqrt(power + 1e-06)
@@ -352,7 +386,7 @@
         stack = None
         for k in range(SEGS):
             first = (k * MINE + s) * ROWS
-            weight = val_ref[k] * recv2_ref[k * MINE + s, pl.ds(8, 1), :]
+            weight = val_ref[k] * src_valid[k * MINE + s : k * MINE + s + 1, :]
             term = lag[first : first + ROWS] * (scale[first : first + ROWS] * weight[:, :1])
             stack = term if stack is None else stack + term
         out_ref[s] = stack
@@ -361,8 +395,8 @@
         copy.wait_send()
 
     for target in range(PLANES):
-        spread(target, 1).wait_send()
-        pl.when(jnp.logical_or(target != z, t != dest))(spread(target, 0).wait_send)
+        for row in range(YROWS):
+            pl.when(apart(target, row))(spread(target, row).wait_send)
 
 
 def local(record, source_channels, valid_mask):
@@ -374,24 +408,29 @@
     return pl.pallas_call(
         kernel,
         out_shape=jax.ShapeDtypeStruct((MINE, ROWS, LAGS), f32),
-        in_specs=[pl.BlockSpec(memory_space=pltpu.SMEM), vmem, vmem, vmem, hbm, hbm],
+        in_specs=[hbm] * 6,
         out_specs=vmem,
         scratch_shapes=[
-            pltpu.VMEM((2, 512, 256), bf16),
-            pltpu.VMEM((2, 2 * NF, LAGS), bf16),
+            pltpu.SMEM((NSRC,), jnp.int32),
+            pltpu.VMEM((1, ROWS), jnp.int32),
+            pltpu.VMEM((ROWS, HALF), f32),
+            pltpu.VMEM(small.shape, f32),
+            pltpu.VMEM(forward.shape, bf16),
+            pltpu.VMEM(inverse.shape, bf16),
             pltpu.VMEM((SEGS + 1, ROWS, HALF), f32),
             pltpu.VMEM((SEGS, ROWS, LANES), f32),
             pltpu.VMEM((ROWS, LANES), f32),
             pltpu.VMEM((9, LANES), f32),
-            pltpu.VMEM((OWNERS, 9, LANES), f32),
+            pltpu.VMEM((COLS, 9, LANES), f32),
             pltpu.VMEM((9, LANES), f32),
-            pltpu.VMEM((SEGS * MINE, 9, LANES), f32),
+            pltpu.VMEM((2, SEGS * MINE, 9, LANES), f32),
             pltpu.VMEM((SEGS, 8, ROWS, 256), f32),
             pltpu.VMEM((8, SEGS * MINE, 256), f32),
             pltpu.VMEM((SEGS * MINE * ROWS, 2 * NF), bf16),
             pltpu.VMEM((SEGS * MINE * ROWS, 2 * NF), bf16),
-            dma((2,)), dma((SEGS,)), dma((SEGS,)), dma((SEGS,)), dma((SEGS,)),
-            dma((OWNERS,)), dma((OWNERS,)), dma((16,)), dma((16,)), pltpu.SemaphoreType.REGULAR((16,)),
+            dma((6,)), dma((SEGS,)), dma((SEGS,)), dma((SEGS,)), dma((SEGS,)),
+            dma((COLS,)), dma((COLS,)), dma((PLANES * YROWS,)), dma((2, SEGS * MINE)),
+            pltpu.SemaphoreType.REGULAR((PLANES * YROWS,)),
         ],
         compiler_params=pltpu.CompilerParams(
             collective_id=0, has_side_effects=True, vmem_limit_bytes=60 * 2**20

time: 29.6 us -> 33.1 us (1.12)
  Pallas kernels: 27.9 us -> 31.5 us
    pallas_call x1, Pallas kernels: 27.9 us -> 31.5 us  [local(): pl.pallas_call(kernel, out_shape=jax.ShapeDtypeStruct((MINE, ROWS, LAGS),...]
where the time goes in v3:
time: 33.1 us; the launch traced here: 33 us
  Pallas kernels  31.5 us (95%)
  local copies, waits for them, and re-layouts  1.47 us (4%)
    pallas_call x1, Pallas kernels, local(): pl.pallas_call(kernel, out_shape=jax.ShapeDtypeStruct((MINE, ROWS, LAGS),...  31.5 us
    unnamed x1, local copies, waits for them, and re-layouts  1.47 us

profile of v3, /device:TPU:9, one launch (start us, length us, event | category | flops | bytes accessed | tf_op | source)
XLA Modules:
  0.0 33.0 jit_solution(11942503497345264703)
XLA Ops:
  0.0 31.5 %correlate.1 = f32[4,16,256]{2,1,0:T(8,128)} custom-call(s32[16]{0:T(128)} %chan_hbm.1, s32[1,16]{1,0:T(1,128)} %bitcast.1, f32[16,1024]{1,0:T(8,128)} %rec_hbm.1, f32[56,128]{1,0:T(8,128)} %constant.6.clone.small_hbm, bf16[2,512,256]{2,1,0:T(8,128)(2,1)} %constant.7.clone.fwd_hbm, bf16[2,2048,256]{2,1,0:T(8,128)(2,1)} %constant.8.clone.inv_hbm), custom_call_target="tpu_custom_call" | custom-call | tf_op jit(solution)/shard_map/correlate/pallas_call | solution.py:408
  31.5 1.5 %copy.8 = f32[4,16,256]{2,1,0:T(8,128)} copy(f32[4,16,256]{2,1,0:T(8,128)} %correlate.1) | data formatting | bytes 131072

commit v4 on v2

--- a/solution.py
+++ b/solution.py
@@ -155,8 +155,8 @@
 
 
 def kernel(
-    chan_ref, mask_ref, rec_ref, small_ref, fwd_hbm, inv_hbm, out_ref,
-    fwd_ref, inv_ref, all_ref, val_ref, vsend_ref, send1_ref, recv1_ref, send2_ref, recv2_ref,
+    chan_hbm, mask_hbm, rec_hbm, small_hbm, fwd_hbm, inv_hbm, out_ref,
+    chan_ref, mask_ref, rec_ref, small_ref, fwd_ref, inv_ref, all_ref, val_ref, vsend_ref, send1_ref, recv1_ref, send2_ref, recv2_ref,
     white_ref, src_ref, high_ref, low_ref,
     tab_sem, rec_ssem, rec_rsem, val_ssem, val_rsem, ssem1, rsem1, ssem2, rsem2, ready_sem,
 ):
@@ -167,10 +167,21 @@
     group = r // OWNERS
     dest = z // 2
 
-    load_fwd = pltpu.make_async_copy(fwd_hbm, fwd_ref, tab_sem.at[0])
-    load_inv = pltpu.make_async_copy(inv_hbm, inv_ref, tab_sem.at[1])
-    load_fwd.start()
-    load_inv.start()
+    loads = [
+        pltpu.make_async_copy(src, dst, tab_sem.at[n])
+        for n, (src, dst) in enumerate(
+            (
+                (rec_hbm, rec_ref),
+                (chan_hbm, chan_ref),
+                (mask_hbm, mask_ref),
+                (small_hbm, small_ref),
+                (fwd_hbm, fwd_ref),
+                (inv_hbm, inv_ref),
+            )
+        )
+    ]
+    for load in loads:
+        load.start()
 
     barrier = pltpu.get_barrier_semaphore()
 
@@ -203,6 +214,8 @@
             for row in rows:
                 greet(target * 16 + row * COLS + x, dest)
 
+    for load in loads[:3]:
+        load.wait()
     rec = rec_ref[...]
     mask = jnp.broadcast_to(mask_ref[...].astype(jnp.float32), (ROWS, ROWS))
     square = (ROWS, ROWS)
@@ -291,7 +304,8 @@
         slot = (t + d) % SEGS
         arrived(all_ref.at[slot], rec_rsem.at[slot])
         arrived(val_ref.at[slot], val_rsem.at[slot])
-    load_fwd.wait()
+    loads[3].wait()
+    loads[4].wait()
     small = small_ref[...]
 
     @pl.loop(0, SEGS)
@@ -344,7 +358,7 @@
                     high_ref[rows, first : first + LANES] = high
                     low_ref[rows, first : first + LANES] = low
 
-    load_inv.wait()
+    loads[5].wait()
     lag = dot3(high_ref[...], low_ref[...], inv_ref[0], inv_ref[1])
     power = jnp.sum(lag * lag, axis=1, keepdims=True) * (1.0 / LAGS)
     scale = lax.rsqrt(power + 1e-06)
@@ -373,12 +387,16 @@
     dma = pltpu.SemaphoreType.DMA
     return pl.pallas_call(
         kernel,
-        out_shape=jax.ShapeDtypeStruct((MINE, ROWS, LAGS), f32),
-        in_specs=[pl.BlockSpec(memory_space=pltpu.SMEM), vmem, vmem, vmem, hbm, hbm],
+        out_shape=pltpu.VMEM((MINE, ROWS, LAGS), f32),
+        in_specs=[hbm] * 6,
         out_specs=vmem,
         scratch_shapes=[
-            pltpu.VMEM((2, 512, 256), bf16),
-            pltpu.VMEM((2, 2 * NF, LAGS), bf16),
+            pltpu.SMEM((NSRC,), jnp.int32),
+            pltpu.VMEM((1, ROWS), jnp.int32),
+            pltpu.VMEM((ROWS, HALF), f32),
+            pltpu.VMEM(small.shape, f32),
+            pltpu.VMEM(forward.shape, bf16),
+            pltpu.VMEM(inverse.shape, bf16),
             pltpu.VMEM((SEGS + 1, ROWS, HALF), f32),
             pltpu.VMEM((SEGS, ROWS, LANES), f32),
             pltpu.VMEM((ROWS, LANES), f32),
@@ -390,7 +408,7 @@
             pltpu.VMEM((8, SEGS * MINE, 256), f32),
             pltpu.VMEM((SEGS * MINE * ROWS, 2 * NF), bf16),
             pltpu.VMEM((SEGS * MINE * ROWS, 2 * NF), bf16),
-            dma((2,)), dma((SEGS,)), dma((SEGS,)), dma((SEGS,)), dma((SEGS,)),
+            dma((6,)), dma((SEGS,)), dma((SEGS,)), dma((SEGS,)), dma((SEGS,)),
             dma((OWNERS,)), dma((OWNERS,)), dma((16,)), dma((16,)), pltpu.SemaphoreType.REGULAR((16,)),
         ],
         compiler_params=pltpu.CompilerParams(

time: 29.6 us -> 27.2 us (0.919)
  Pallas kernels: 27.9 us -> 26.5 us
  local copies, waits for them, and re-layouts: 1.47 us -> 0.63 us
    pallas_call x1, Pallas kernels: 27.9 us -> 26.5 us  [local(): pl.pallas_call(kernel, out_shape=pltpu.VMEM((MINE, ROWS, LAGS), f32), in_...]
    unnamed x1, local copies, waits for them, and re-layouts: 1.47 us -> 0.63 us
where the time goes in v4:
time: 27.2 us; the launch traced here: 27.1 us
  Pallas kernels  26.5 us (97%)
  local copies, waits for them, and re-layouts  0.63 us (2%)
    pallas_call x1, Pallas kernels, local(): pl.pallas_call(kernel, out_shape=pltpu.VMEM((MINE, ROWS, LAGS), f32), in_...  26.5 us
    unnamed x1, local copies, waits for them, and re-layouts  0.63 us

profile of v4, /device:TPU:9, one launch (start us, length us, event | category | flops | bytes accessed | tf_op | source)
XLA Modules:
  0.0 27.1 jit_solution(16229463009108283166)
XLA Ops:
  0.0 26.5 %correlate.1 = f32[4,16,256]{2,1,0:T(8,128)S(1)} custom-call(s32[16]{0:T(128)} %chan_hbm.1, s32[1,16]{1,0:T(1,128)} %bitcast.1, f32[16,1024]{1,0:T(8,128)} %rec_hbm.1, f32[56,128]{1,0:T(8,128)} %constant.6.clone.small_hbm, bf16[2,512,256]{2,1,0:T(8,128)(2,1)} %constant.7.clone.fwd_hbm, bf16[2,2048,256]{2,1,0:T(8,128)(2,1)} %constant.8.clone.inv_hbm), custom_call_target="tpu_custom_call" | custom-call | tf_op jit(solution)/shard_map/correlate/pallas_call | solution.py:388
  26.5 0.6 %copy.8 = f32[4,16,256]{2,1,0:T(8,128)} copy(f32[4,16,256]{2,1,0:T(8,128)S(1)} %correlate.1) | data formatting | bytes 131072

commit v5 on v4

--- a/solution.py
+++ b/solution.py
@@ -157,7 +157,7 @@
 def kernel(
     chan_hbm, mask_hbm, rec_hbm, small_hbm, fwd_hbm, inv_hbm, out_ref,
     chan_ref, mask_ref, rec_ref, small_ref, fwd_ref, inv_ref, all_ref, val_ref, vsend_ref, send1_ref, recv1_ref, send2_ref, recv2_ref,
-    white_ref, src_ref, high_ref, low_ref,
+    white_ref, src_ref,
     tab_sem, rec_ssem, rec_rsem, val_ssem, val_rsem, ssem1, rsem1, ssem2, rsem2, ready_sem,
 ):
     r = lax.axis_index("recv")
@@ -342,24 +342,25 @@
         src_ref[j, :, :LANES] = re[j]
         src_ref[j, :, LANES:] = im[j]
 
-    @pl.loop(0, SEGS)
-    def _(k):
-        for j in range(8):
+    def cross(j):
+        highs, lows = [], []
+        for k in range(SEGS):
             rec_re, rec_im = white_ref[k, j, :, :LANES], white_ref[k, j, :, LANES:]
             for s in range(MINE):
                 src = src_ref[j, pl.ds(k * MINE + s, 1), :]
                 src_re, src_im = src[:, :LANES], src[:, LANES:]
-                cross_re = src_re * rec_re + src_im * rec_im
-                cross_im = src_re * rec_im - src_im * rec_re
-                rows = pl.ds(pl.multiple_of(k * (MINE * ROWS), MINE * ROWS) + s * ROWS, ROWS)
-                for part, value in enumerate((cross_re, cross_im)):
-                    high, low = halves(value)
-                    first = (2 * j + part) * LANES
-                    high_ref[rows, first : first + LANES] = high
-                    low_ref[rows, first : first + LANES] = low
+                parts = halves(src_re * rec_re + src_im * rec_im), halves(src_re * rec_im - src_im * rec_re)
+                highs.append(jnp.concatenate([p[0] for p in parts], axis=1))
+                lows.append(jnp.concatenate([p[1] for p in parts], axis=1))
+        return jnp.concatenate(highs, axis=0), jnp.concatenate(lows, axis=0)
 
     loads[5].wait()
-    lag = dot3(high_ref[...], low_ref[...], inv_ref[0], inv_ref[1])
+    lag = None
+    for j in range(8):
+        high, low = cross(j)
+        block = pl.ds(j * 256, 256)
+        term = dot3(high, low, inv_ref[0, block, :], inv_ref[1, block, :])
+        lag = term if lag is None else lag + term
     power = jnp.sum(lag * lag, axis=1, keepdims=True) * (1.0 / LAGS)
     scale = lax.rsqrt(power + 1e-06)
     for s in range(MINE):
@@ -406,8 +407,6 @@
             pltpu.VMEM((SEGS * MINE, 9, LANES), f32),
             pltpu.VMEM((SEGS, 8, ROWS, 256), f32),
             pltpu.VMEM((8, SEGS * MINE, 256), f32),
-            pltpu.VMEM((SEGS * MINE * ROWS, 2 * NF), bf16),
-            pltpu.VMEM((SEGS * MINE * ROWS, 2 * NF), bf16),
             dma((6,)), dma((SEGS,)), dma((SEGS,)), dma((SEGS,)), dma((SEGS,)),
             dma((OWNERS,)), dma((OWNERS,)), dma((16,)), dma((16,)), pltpu.SemaphoreType.REGULAR((16,)),
         ],

time: 27.2 us -> 26.5 us (0.974)
  Pallas kernels: 26.5 us -> 25.7 us
    pallas_call x1, Pallas kernels: 26.5 us -> 25.7 us  [local(): pl.pallas_call(kernel, out_shape=pltpu.VMEM((MINE, ROWS, LAGS), f32), in_...]
where the time goes in v5:
time: 26.5 us; the launch traced here: 26.4 us
  Pallas kernels  25.7 us (97%)
  local copies, waits for them, and re-layouts  0.63 us (2%)
    pallas_call x1, Pallas kernels, local(): pl.pallas_call(kernel, out_shape=pltpu.VMEM((MINE, ROWS, LAGS), f32), in_...  25.7 us
    unnamed x1, local copies, waits for them, and re-layouts  0.63 us

profile of v5, /device:TPU:9, one launch (start us, length us, event | category | flops | bytes accessed | tf_op | source)
XLA Modules:
  0.0 26.4 jit_solution(13956488296592937625)
XLA Ops:
  0.0 25.7 %correlate.1 = f32[4,16,256]{2,1,0:T(8,128)S(1)} custom-call(s32[16]{0:T(128)} %chan_hbm.1, s32[1,16]{1,0:T(1,128)} %bitcast.1, f32[16,1024]{1,0:T(8,128)} %rec_hbm.1, f32[56,128]{1,0:T(8,128)} %constant.6.clone.small_hbm, bf16[2,512,256]{2,1,0:T(8,128)(2,1)} %constant.7.clone.fwd_hbm, bf16[2,2048,256]{2,1,0:T(8,128)(2,1)} %constant.8.clone.inv_hbm), custom_call_target="tpu_custom_call" | custom-call | tf_op jit(solution)/shard_map/correlate/pallas_call | solution.py:389
  25.8 0.6 %copy.8 = f32[4,16,256]{2,1,0:T(8,128)} copy(f32[4,16,256]{2,1,0:T(8,128)S(1)} %correlate.1) | data formatting | bytes 131072

commit v6 on v5

--- a/solution.py
+++ b/solution.py
@@ -326,6 +326,13 @@
                 pl.semaphore_wait(ready_sem.at[2 * target + flip], 1)
                 spread(target, flip).start()
 
+    for copy in sends:
+        copy.wait_send()
+
+    for target in range(PLANES):
+        spread(target, 1).wait_send()
+        pl.when(jnp.logical_or(target != z, t != dest))(spread(target, 0).wait_send)
+
     for e in range(SEGS * MINE):
         b, p, h = e // MINE, (e % MINE) // 2, e % 2
         own = jnp.logical_and(jnp.logical_and(t == b, z == 2 * t + p), yh // 2 == h)
@@ -342,11 +349,11 @@
         src_ref[j, :, :LANES] = re[j]
         src_ref[j, :, LANES:] = im[j]
 
-    def cross(j):
+    def cross(j, first):
         highs, lows = [], []
         for k in range(SEGS):
             rec_re, rec_im = white_ref[k, j, :, :LANES], white_ref[k, j, :, LANES:]
-            for s in range(MINE):
+            for s in range(first, first + 2):
                 src = src_ref[j, pl.ds(k * MINE + s, 1), :]
                 src_re, src_im = src[:, :LANES], src[:, LANES:]
                 parts = halves(src_re * rec_re + src_im * rec_im), halves(src_re * rec_im - src_im * rec_re)
@@ -355,29 +362,23 @@
         return jnp.concatenate(highs, axis=0), jnp.concatenate(lows, axis=0)
 
     loads[5].wait()
-    lag = None
-    for j in range(8):
-        high, low = cross(j)
-        block = pl.ds(j * 256, 256)
-        term = dot3(high, low, inv_ref[0, block, :], inv_ref[1, block, :])
-        lag = term if lag is None else lag + term
-    power = jnp.sum(lag * lag, axis=1, keepdims=True) * (1.0 / LAGS)
-    scale = lax.rsqrt(power + 1e-06)
-    for s in range(MINE):
-        stack = None
-        for k in range(SEGS):
-            first = (k * MINE + s) * ROWS
-            weight = val_ref[k] * recv2_ref[k * MINE + s, pl.ds(8, 1), :]
-            term = lag[first : first + ROWS] * (scale[first : first + ROWS] * weight[:, :1])
-            stack = term if stack is None else stack + term
-        out_ref[s] = stack
-
-    for copy in sends:
-        copy.wait_send()
-
-    for target in range(PLANES):
-        spread(target, 1).wait_send()
-        pl.when(jnp.logical_or(target != z, t != dest))(spread(target, 0).wait_send)
+    for first in (0, 2):
+        lag = None
+        for j in range(8):
+            high, low = cross(j, first)
+            block = pl.ds(j * 256, 256)
+            term = dot3(high, low, inv_ref[0, block, :], inv_ref[1, block, :])
+            lag = term if lag is None else lag + term
+        power = jnp.sum(lag * lag, axis=1, keepdims=True) * (1.0 / LAGS)
+        scale = lax.rsqrt(power + 1e-06)
+        for s in range(2):
+            stack = None
+            for k in range(SEGS):
+                row = (2 * k + s) * ROWS
+                weight = val_ref[k] * recv2_ref[k * MINE + first + s, pl.ds(8, 1), :]
+                term = lag[row : row + ROWS] * (scale[row : row + ROWS] * weight[:, :1])
+                stack = term if stack is None else stack + term
+            out_ref[first + s] = stack
 
 
 def local(record, source_channels, valid_mask):

time: 26.5 us -> 26.3 us (level)
  no operation moved by 1% of the time
where the time goes in v6:
time: 26.3 us; the launch traced here: 26.2 us
  Pallas kernels  25.6 us (97%)
  local copies, waits for them, and re-layouts  0.63 us (2%)
    pallas_call x1, Pallas kernels, local(): pl.pallas_call(kernel, out_shape=pltpu.VMEM((MINE, ROWS, LAGS), f32), in_...  25.6 us
    unnamed x1, local copies, waits for them, and re-layouts  0.63 us

profile of v6, /device:TPU:9, one launch (start us, length us, event | category | flops | bytes accessed | tf_op | source)
XLA Modules:
  0.0 26.2 jit_solution(7853328198453864222)
XLA Ops:
  0.0 25.6 %correlate.1 = f32[4,16,256]{2,1,0:T(8,128)S(1)} custom-call(s32[16]{0:T(128)} %chan_hbm.1, s32[1,16]{1,0:T(1,128)} %bitcast.1, f32[16,1024]{1,0:T(8,128)} %rec_hbm.1, f32[56,128]{1,0:T(8,128)} %constant.6.clone.small_hbm, bf16[2,512,256]{2,1,0:T(8,128)(2,1)} %constant.7.clone.fwd_hbm, bf16[2,2048,256]{2,1,0:T(8,128)(2,1)} %constant.8.clone.inv_hbm), custom_call_target="tpu_custom_call" | custom-call | tf_op jit(solution)/shard_map/correlate/pallas_call | solution.py:390
  25.6 0.6 %copy.8 = f32[4,16,256]{2,1,0:T(8,128)} copy(f32[4,16,256]{2,1,0:T(8,128)S(1)} %correlate.1) | data formatting | bytes 131072

commit v7 on v6

--- a/solution.py
+++ b/solution.py
@@ -259,6 +259,34 @@
         )
         copy.start()
         sends.append(copy)
+    def arrived(buf, sem):
+        pltpu.make_async_remote_copy(
+            buf, buf, sem, sem, device_id={"recv": r, "tm": t}, device_id_type=MESH
+        ).wait_recv()
+
+    for d in range(1, OWNERS):
+        slot = (cand + d) % OWNERS
+        arrived(recv1_ref.at[slot], rsem1.at[slot])
+
+    owner = jnp.clip((chan_ref[group] - group * (OWNERS * ROWS)) // ROWS, 0, OWNERS - 1)
+    chosen = recv1_ref[owner]
+    send2_ref[...] = chosen
+    entry = t * MINE + (z % 2) * 2 + yh // 2
+
+    @pl.when(t == dest)
+    def _():
+        recv2_ref[entry] = chosen
+
+    def spread(target, flip):
+        return pltpu.make_async_remote_copy(
+            send2_ref, recv2_ref.at[entry], ssem2.at[2 * target + flip], rsem2.at[entry],
+            device_id={"recv": target * 16 + rows[flip] * COLS + x, "tm": dest}, device_id_type=MESH,
+        )
+
+    for target in range(PLANES):
+        pl.when(target <= z)(spread(target, 1).start)
+        pl.when(jnp.logical_or(target < z, jnp.logical_and(target == z, t != dest)))(spread(target, 0).start)
+
     for d in range(1, SEGS):
         to = {"recv": r, "tm": (t + d) % SEGS}
         copy = pltpu.make_async_remote_copy(
@@ -271,34 +299,6 @@
         )
         copy.start()
         sends.append(copy)
-
-    def arrived(buf, sem):
-        pltpu.make_async_remote_copy(
-            buf, buf, sem, sem, device_id={"recv": r, "tm": t}, device_id_type=MESH
-        ).wait_recv()
-
-    for d in range(1, OWNERS):
-        slot = (cand + d) % OWNERS
-        arrived(recv1_ref.at[slot], rsem1.at[slot])
-
-    owner = jnp.clip((chan_ref[group] - group * (OWNERS * ROWS)) // ROWS, 0, OWNERS - 1)
-    chosen = recv1_ref[owner]
-    send2_ref[...] = chosen
-    entry = t * MINE + (z % 2) * 2 + yh // 2
-
-    @pl.when(t == dest)
-    def _():
-        recv2_ref[entry] = chosen
-
-    def spread(target, flip):
-        return pltpu.make_async_remote_copy(
-            send2_ref, recv2_ref.at[entry], ssem2.at[2 * target + flip], rsem2.at[entry],
-            device_id={"recv": target * 16 + rows[flip] * COLS + x, "tm": dest}, device_id_type=MESH,
-        )
-
-    for target in range(PLANES):
-        pl.when(target <= z)(spread(target, 1).start)
-        pl.when(jnp.logical_or(target < z, jnp.logical_and(target == z, t != dest)))(spread(target, 0).start)
 
     for d in range(1, SEGS):
         slot = (t + d) % SEGS

time: 26.3 us -> 26.4 us (level)
  no operation moved by 1% of the time
where the time goes in v7:
time: 26.4 us; the launch traced here: 26.2 us
  Pallas kernels  25.6 us (97%)
  local copies, waits for them, and re-layouts  0.63 us (2%)
    pallas_call x1, Pallas kernels, local(): pl.pallas_call(kernel, out_shape=pltpu.VMEM((MINE, ROWS, LAGS), f32), in_...  25.6 us
    unnamed x1, local copies, waits for them, and re-layouts  0.63 us

profile of v7, /device:TPU:9, one launch (start us, length us, event | category | flops | bytes accessed | tf_op | source)
XLA Modules:
  0.0 26.2 jit_solution(8685703998309998943)
XLA Ops:
  0.0 25.6 %correlate.1 = f32[4,16,256]{2,1,0:T(8,128)S(1)} custom-call(s32[16]{0:T(128)} %chan_hbm.1, s32[1,16]{1,0:T(1,128)} %bitcast.1, f32[16,1024]{1,0:T(8,128)} %rec_hbm.1, f32[56,128]{1,0:T(8,128)} %constant.6.clone.small_hbm, bf16[2,512,256]{2,1,0:T(8,128)(2,1)} %constant.7.clone.fwd_hbm, bf16[2,2048,256]{2,1,0:T(8,128)(2,1)} %constant.8.clone.inv_hbm), custom_call_target="tpu_custom_call" | custom-call | tf_op jit(solution)/shard_map/correlate/pallas_call | solution.py:390
  25.6 0.6 %copy.8 = f32[4,16,256]{2,1,0:T(8,128)} copy(f32[4,16,256]{2,1,0:T(8,128)S(1)} %correlate.1) | data formatting | bytes 131072

commit v8 on v7

--- a/solution.py
+++ b/solution.py
@@ -189,7 +189,8 @@
         pl.semaphore_signal(barrier, inc=1, device_id={"recv": recv, "tm": tm}, device_id_type=MESH)
 
     rows = (yh, 3 - yh)
-    for d in range(1, OWNERS):
+    far_first = (6, 5, 7, 2, 4, 1, 3)
+    for d in far_first:
         greet(group * OWNERS + (cand + d) % OWNERS, t)
     for d in range(1, SEGS):
         greet(r, (t + d) % SEGS)
@@ -252,7 +253,7 @@
                     )
 
     sends = []
-    for d in range(1, OWNERS):
+    for d in far_first:
         copy = pltpu.make_async_remote_copy(
             send1_ref, recv1_ref.at[cand], ssem1.at[d], rsem1.at[cand],
             device_id={"recv": group * OWNERS + (cand + d) % OWNERS, "tm": t}, device_id_type=MESH,

time: 26.4 us -> 26.4 us (level)
  no operation moved by 1% of the time
where the time goes in v8:
time: 26.4 us; the launch traced here: 26.3 us
  Pallas kernels  25.7 us (97%)
  local copies, waits for them, and re-layouts  0.63 us (2%)
    pallas_call x1, Pallas kernels, local(): pl.pallas_call(kernel, out_shape=pltpu.VMEM((MINE, ROWS, LAGS), f32), in_...  25.7 us
    unnamed x1, local copies, waits for them, and re-layouts  0.63 us

profile of v8, /device:TPU:9, one launch (start us, length us, event | category | flops | bytes accessed | tf_op | source)
XLA Modules:
  0.0 26.3 jit_solution(10096366438872595704)
XLA Ops:
  0.0 25.7 %correlate.1 = f32[4,16,256]{2,1,0:T(8,128)S(1)} custom-call(s32[16]{0:T(128)} %chan_hbm.1, s32[1,16]{1,0:T(1,128)} %bitcast.1, f32[16,1024]{1,0:T(8,128)} %rec_hbm.1, f32[56,128]{1,0:T(8,128)} %constant.6.clone.small_hbm, bf16[2,512,256]{2,1,0:T(8,128)(2,1)} %constant.7.clone.fwd_hbm, bf16[2,2048,256]{2,1,0:T(8,128)(2,1)} %constant.8.clone.inv_hbm), custom_call_target="tpu_custom_call" | custom-call | tf_op jit(solution)/shard_map/correlate/pallas_call | solution.py:391
  25.7 0.6 %copy.8 = f32[4,16,256]{2,1,0:T(8,128)} copy(f32[4,16,256]{2,1,0:T(8,128)S(1)} %correlate.1) | data formatting | bytes 131072
